TPU v7x, 32 devices: a whole 2x2x4 slice. The times are simulated.
32 devices in a mesh: lat: 8 (over z, y), lon: 4 (over x, core).
Axes of the slice: x: 2, y: 2, z: 4, core: 2. Of those that a mesh axis runs over, the one named last changes fastest.
Arguments:
- grid_fields: bfloat16 [1280, 50, 3, 2560], P('lat', None, None, 'lon'), may hold values from -6 to 6
- legendre: bfloat16 [512, 1280, 640], P(('lat', 'lon')), may hold values from -0.15625 to 0.15625
- wave_of_slot: int32 [512], replicated, may hold values from 0 to 511, as said below
- energy_weight: float32 [3, 640], replicated, may hold values from 0.1 to 10
Outputs:
- spectral: bfloat16 [50, 3, 512, 2, 640], P(None, None, ('lat', 'lon'))
- gram_matrix: float32 [50, 50], replicated
Inputs may be any that keep to these rules, and one draw needn't show every extreme that they name: `wave_of_slot`: every wavenumber 0 to 511 stands in exactly one slot; slot d * 16 + r holds a wavenumber of r * 32 to r * 32 + 31.
All inputs are finite; a program needn't handle non-finite values.
Results may differ from a plain program's by a relative error of at most 0.0043.
Values may be sent and summed in bfloat16 or wider, within the bound.
No kernel may reach another device: no remote copies, remote signals or barrier semaphores. Data moves between devices by JAX's collectives and lax.ppermute only.
A program may use at most 256 MiB of HBM per device.

v0:
```python
import math
import jax
import jax.numpy as jnp
from jax import lax
from jax.sharding import PartitionSpec as P

M = 512
NT = 640
LEV = 3


def make_trig(wave_list, lon_total):
    longitude = jnp.arange(lon_total, dtype=jnp.int32)
    phase_index = longitude[:, None] * wave_list[None, :] % lon_total
    angles = phase_index.astype(jnp.float32) * (2.0 * math.pi / lon_total)
    stacked = jnp.stack([jnp.cos(angles), -jnp.sin(angles)], axis=2)
    return stacked.reshape(lon_total, 2 * wave_list.shape[0]).astype(jnp.bfloat16)


def on_device(grid_fields, legendre, wave_of_slot, energy_weight):
    lat_dev, vectors, levels, lon_dev = grid_fields.shape
    bands = lax.axis_size("lat")
    sectors = lax.axis_size("lon")
    lon_total = lon_dev * sectors
    per_dev = legendre.shape[0]
    degrees = legendre.shape[2]
    fields = vectors * levels
    band_rows = lat_dev // sectors
    norm_scale = 1.0 / math.sqrt(lon_total)
    trig_table = make_trig(wave_of_slot, lon_total)
    moved_rows = lax.all_to_all(grid_fields, "lon", split_axis=0, concat_axis=3, tiled=True)
    product = jnp.dot(
        moved_rows.reshape(-1, lon_total), trig_table, preferred_element_type=jnp.float32
    )
    fourier = product.reshape(band_rows, fields, -1) * norm_scale
    gathered = lax.all_to_all(
        lax.all_to_all(fourier, "lat", split_axis=2, concat_axis=0, tiled=True),
        "lon",
        split_axis=2,
        concat_axis=0,
        tiled=True,
    )
    cols_here = gathered.shape[2]
    columns = gathered.reshape(sectors, bands, band_rows, fields, cols_here).transpose(
        1, 0, 2, 3, 4
    )
    columns = columns.reshape(bands * lat_dev, fields, cols_here)
    columns = columns.reshape(bands * lat_dev, fields, per_dev, 2)
    device_slot = (lax.axis_index("lat") * sectors + lax.axis_index("lon")) * per_dev
    own_waves = lax.dynamic_slice_in_dim(wave_of_slot, device_slot, per_dev, 0)
    degree_index = jnp.arange(degrees, dtype=jnp.int32)
    tri_mask = (degree_index[None, :] >= own_waves[:, None]).astype(jnp.float32)
    legendre_table = legendre.astype(jnp.float32) * tri_mask[:, None, :]
    spectral = jnp.einsum(
        "aftp,tan->ftpn", columns, legendre_table, precision=lax.Precision.HIGHEST
    )
    spectral = spectral.reshape(vectors, levels, per_dev, 2, degrees)
    factor = jnp.where(own_waves == 0, 1.0, 2.0).astype(jnp.float32)
    weighted = spectral * factor[None, None, :, None, None] * energy_weight[None, :, None, None, :]
    partial_value = jnp.dot(
        spectral.reshape(vectors, -1),
        weighted.reshape(vectors, -1).T,
        precision=lax.Precision.HIGHEST,
    )
    gram_matrix = lax.psum(partial_value, ("lat", "lon")) / (LEV * M * NT)
    return (spectral.astype(jnp.bfloat16), gram_matrix)


def solution(mesh):
    placed = (P("lat", None, None, "lon"), P(("lat", "lon"), None, None), P(), P())
    return jax.shard_map(
        on_device,
        mesh=mesh,
        in_specs=placed,
        out_specs=(P(None, None, ("lat", "lon"), None, None), P()),
        check_vma=False,
    )
```

profile of v0, /device:TPU:0, one launch (start us, length us, event | category | flops | bytes accessed | tf_op | source)
XLA Modules:
  0.0 2192.7 jit_solution(3052948345299898282)
XLA Ops:
  0.6 22.1 %copy.47 = bf16[160,50,3,640]{3,1,2,0:T(8,128)(2,1)} copy(bf16[160,50,3,640]{3,0,2,1:T(8,128)(2,1)} %param.4) | data formatting | bytes 61440000 | tf_op args[0]
  22.7 0.0 copy-start.1
  22.7 10.0 all-to-all-start
  32.8 0.0 copy-done.1
  32.8 22.3 %cosine_convert_fusion = (bf16[2560,512,1]{1,0,2:T(8,128)(2,1)S(1)}, bf16[2560,512,1]{1,0,2:T(8,128)(2,1)S(1)}) fusion(s32[512]{0:T(512)S(1)} %copy-done.1), kind=kLoop, calls=%fused_computation.14 | loop fusion | flops 15728640 | bytes 5244928 | tf_op jit(solution)/shard_map/convert
  55.0 2.8 pad_maximum_fusion
  57.9 13.9 copy.46
  71.8 11.6 convert_element_type.43
  83.4 321.9 %all-to-all-done = bf16[160,50,3,640]{3,1,2,0:T(8,128)(2,1)} async-done(((bf16[160,50,3,640]{3,1,2,0:T(8,128)(2,1)}), bf16[160,50,3,640]{3,1,2,0:T(8,128)(2,1)}, u32[]{:S(2)}, u32[]{:S(2)}) %all-to-all-start) | async-done | bytes 30720032 | tf_op jit(solution)/shard_map/all_to_all | solution.py:31
  405.4 27.3 %copy.48 = bf16[4,40,50,3,640]{4,0,3,2,1:T(4,128)(2,1)} copy(bf16[4,40,50,3,640]{4,2,3,1,0:T(8,128)(2,1)} %bitcast.2) | data formatting | bytes 61440000 | tf_op jit(solution)/shard_map/all_to_all | solution.py:31
  432.6 21.6 copy.67
  454.2 39.4 %multiply_bitcast_fusion = f32[6000,1024]{1,0:T(8,128)} fusion(bf16[2560,1024]{0,1:T(8,128)(2,1)} %convert_element_type.43, bf16[6000,2560]{1,0:T(8,128)(2,1)} %bitcast.48), kind=kOutput, calls=%fused_computation.5 | convolution fusion | flops 31463424000 | bytes 60538880 | tf_op jit(solution)/shard_map/dot_general | solution.py:32
  493.6 19.6 mul.105
  513.3 43.6 %copy.49 = f32[40,150,1024]{1,0,2:T(8,128)} copy(f32[40,150,1024]{2,1,0:T(8,128)} %mul.105) | data formatting | bytes 49152000 | tf_op jit(solution)/shard_map/mul | solution.py:35
  556.9 915.7 %all_to_all.48 = f32[40,150,1024]{1,0,2:T(8,128)} all-to-all(f32[40,150,1024]{1,0,2:T(8,128)} %copy.49), channel_id=1, replica_groups=mesh['lat'=8,'lon'=4] {'lat'}, dimensions={2} | all-to-all | bytes 49152000 | tf_op jit(solution)/shard_map/all_to_all | solution.py:37
  1472.6 36.6 %copy.51 = f32[8,40,150,128]{3,1,0,2:T(8,128)} copy(f32[8,40,150,128]{2,1,3,0:T(8,128)} %bitcast.44) | data formatting | bytes 49152000 | tf_op jit(solution)/shard_map/all_to_all | solution.py:37
  1509.2 28.0 %copy.52 = f32[320,150,128]{0,1,2:T(8,128)} copy(f32[320,150,128]{2,0,1:T(8,128)} %bitcast.47) | data formatting | bytes 49152000 | tf_op jit(solution)/shard_map/all_to_all | solution.py:37
  1537.2 0.0 copy-start
  1537.2 9.6 all-to-all-start.2
  1546.8 0.0 copy-done
  1546.9 0.1 mul.108
  1546.9 0.2 mul.109
  1547.1 0.8 compare_select_fusion
  1547.9 0.1 fusion.11
  1548.0 322.3 %all-to-all-done.2 = f32[320,150,128]{0,1,2:T(8,128)} async-done(((f32[320,150,128]{0,1,2:T(8,128)}), f32[320,150,128]{0,1,2:T(8,128)}, u32[]{:S(2)}, u32[]{:S(2)}) %all-to-all-start.2) | async-done | bytes 24576032 | tf_op jit(solution)/shard_map/all_to_all | solution.py:36
  1870.3 46.2 %copy.54 = f32[4,320,150,32]{2,3,1,0:T(8,128)} copy(f32[4,320,150,32]{1,2,3,0:T(8,128)} %bitcast.11) | data formatting | bytes 49152000 | tf_op jit(solution)/shard_map/all_to_all | solution.py:36
  1916.5 39.3 %copy.55 = f32[8,4,40,150,32]{3,2,1,0,4:T(8,128)} copy(f32[8,4,40,150,32]{3,4,2,0,1:T(8,128)} %bitcast.45) | data formatting | bytes 49152000 | tf_op jit(solution)/shard_map/transpose | solution.py:44
  1955.7 76.5 %fusion = f32[16,640,150,2]{1,2,3,0:T(8,128)} fusion(f32[1280,150,16,2]{1,0,3,2:T(8,128)} %bitcast.43, bf16[16,1280,640]{2,1,0:T(8,128)(2,1)} %param.5, f32[16,640]{1,0:T(8,128)S(1)} %fusion.11), kind=kOutput, calls=%fused_computation | convolution fusion | flops 47212134400 | bytes 63119360 | tf_op jit(solution)/shard_map/aftp,tan->ftpn/dot_general | solution.py:54
  2032.2 8.0 copy.70
  2040.3 11.4 copy.60
  2051.6 22.5 %copy.58 = f32[150,16,2,640]{3,2,1,0:T(2,128)} copy(f32[150,16,2,640]{3,0,2,1:T(8,128)} %bitcast.42) | data formatting | bytes 24576000 | tf_op jit(solution)/shard_map/aftp,tan->ftpn/transpose | solution.py:54
  2074.1 15.4 reshape_reshape.7
  2089.5 13.2 fusion.5
  2102.6 18.4 copy.59
  2121.0 15.1 mul.112
  2136.1 16.4 fusion.12
  2152.5 39.1 %psum.7 = f32[50,50]{1,0:T(8,128)S(1)} all-reduce(f32[50,50]{1,0:T(8,128)S(1)} %fusion.12), channel_id=1, replica_groups=mesh['lat'=8,'lon'=4] {'lat','lon'}, use_global_device_ids=true, to_apply=%region_0.1 | all-reduce | flops 2500 | bytes 20000 | tf_op jit(solution)/shard_map/psum | solution.py:65
  2191.6 0.6 broadcast_multiply_fusion
Async XLA Ops:
  22.7 10.0 copy-start.1
  22.7 382.6 %all-to-all-start = ((bf16[160,50,3,640]{3,1,2,0:T(8,128)(2,1)}), bf16[160,50,3,640]{3,1,2,0:T(8,128)(2,1)}, u32[]{:S(2)}, u32[]{:S(2)}) async-start(bf16[160,50,3,640]{3,1,2,0:T(8,128)(2,1)} %copy.47), calls=%async_computation | async-start | bytes 68812800 | tf_op jit(solution)/shard_map/all_to_all | solution.py:31
  1537.2 9.7 copy-start
  1537.2 333.1 %all-to-all-start.2 = ((f32[320,150,128]{0,1,2:T(8,128)}), f32[320,150,128]{0,1,2:T(8,128)}, u32[]{:S(2)}, u32[]{:S(2)}) async-start(f32[320,150,128]{0,1,2:T(8,128)} %copy.52), calls=%async_computation.2 | async-start | bytes 59768832 | tf_op jit(solution)/shard_map/all_to_all | solution.py:36
where the time goes:
time: 2210 us; the launch traced here: 2190 us
  blocking collectives  955 us (43%)
  waiting for transfers between devices  644 us (29%)
  local copies, waits for them, and re-layouts  401 us (18%)
  matrix products  132 us (6%)
  other arithmetic  39.7 us (2%)
    all_to_all x1, blocking collectives, on_device(): lax.all_to_all(fourier, 'lat', split_axis=2, concat_axis=0, tiled=True)  916 us
    all_to_all x1, waiting for transfers between devices, on_device(): lax.all_to_all(lax.all_to_all(fourier, 'lat', split_axis=2, concat_axis=0...  322 us
    all_to_all x1, waiting for transfers between devices, on_device(): lax.all_to_all(grid_fields, 'lon', split_axis=0, concat_axis=3, tiled=True)  322 us
    dot_general x1, matrix products, on_device(): jnp.einsum('aftp,tan->ftpn', columns, legendre_table, precision=lax.Preci...  76.5 us
    all_to_all x2, local copies, waits for them, and re-layouts, on_device(): lax.all_to_all(fourier, 'lat', split_axis=2, concat_axis=0, tiled=True)  64.6 us
    mul x2, local copies, waits for them, and re-layouts, on_device(): fourier = product.reshape(band_rows, fields, -1) * norm_scale  63.2 us
    unnamed x7, local copies, waits for them, and re-layouts  55 us
    all_to_all x1, local copies, waits for them, and re-layouts, on_device(): lax.all_to_all(lax.all_to_all(fourier, 'lat', split_axis=2, concat_axis=0...  46.2 us
  transfers between devices with their start and end apart: 2, of which 2 were waited for; matrix products, arithmetic and copies ran while one was open for 2% of the time, Pallas kernels for 0%

commit v1 on v0

--- a/solution.py
+++ b/solution.py
@@ -33,12 +33,20 @@
         moved_rows.reshape(-1, lon_total), trig_table, preferred_element_type=jnp.float32
     )
     fourier = product.reshape(band_rows, fields, -1) * norm_scale
-    gathered = lax.all_to_all(
-        lax.all_to_all(fourier, "lat", split_axis=2, concat_axis=0, tiled=True),
-        "lon",
-        split_axis=2,
-        concat_axis=0,
-        tiled=True,
+    gathered = jnp.concatenate(
+        lax.all_to_all(
+            jnp.stack(
+                jnp.split(
+                    lax.all_to_all(fourier, "lat", split_axis=2, concat_axis=0, tiled=True),
+                    lax.axis_size("lon"),
+                    axis=2,
+                )
+            ),
+            "lon",
+            0,
+            0,
+        ),
+        axis=0,
     )
     cols_here = gathered.shape[2]
     columns = gathered.reshape(sectors, bands, band_rows, fields, cols_here).transpose(

time: 2210 us -> 2330 us (1.054)
  local copies, waits for them, and re-layouts: 401 us -> 506 us
    another operation x0 -> x5, local copies, waits for them, and re-layouts: none -> 132 us  [on_device(): jnp.stack(jnp.split(lax.all_to_all(fourier, 'lat', split_axis=2, concat_a...]
    all_to_all x2 -> x1, local copies, waits for them, and re-layouts: 64.6 us -> 36.6 us  [on_device(): lax.all_to_all(fourier, 'lat', split_axis=2, concat_axis=0, tiled=True)]
where the time goes in v1:
time: 2330 us; the launch traced here: 2310 us
  blocking collectives  955 us (41%)
  waiting for transfers between devices  640 us (27%)
  local copies, waits for them, and re-layouts  506 us (22%)
  matrix products  133 us (6%)
  other arithmetic  60.3 us (3%)
    all_to_all x1, blocking collectives, on_device(): lax.all_to_all(fourier, 'lat', split_axis=2, concat_axis=0, tiled=True)  916 us
    all_to_all x1, waiting for transfers between devices, on_device(): lax.all_to_all(grid_fields, 'lon', split_axis=0, concat_axis=3, tiled=True)  322 us
    all_to_all x1, waiting for transfers between devices, on_device(): lax.all_to_all(jnp.stack(jnp.split(lax.all_to_all(fourier, 'lat', split_a...  318 us
    another operation x5, local copies, waits for them, and re-layouts, on_device(): jnp.stack(jnp.split(lax.all_to_all(fourier, 'lat', split_axis=2, concat_a...  132 us
    dot_general x1, matrix products, on_device(): jnp.einsum('aftp,tan->ftpn', columns, legendre_table, precision=lax.Preci...  76.9 us
    mul x2, local copies, waits for them, and re-layouts, on_device(): fourier = product.reshape(band_rows, fields, -1) * norm_scale  63.2 us
    unnamed x7, local copies, waits for them, and re-layouts  53.7 us
  transfers between devices with their start and end apart: 2, of which 2 were waited for; matrix products, arithmetic and copies ran while one was open for 2% of the time, Pallas kernels for 0%

profile of v1, /device:TPU:0, one launch (start us, length us, event | category | flops | bytes accessed | tf_op | source)
XLA Modules:
  0.0 2313.7 jit_solution(3045876017830567920)
XLA Ops:
  0.6 22.1 copy.50
  22.7 0.0 copy-start.1
  22.7 10.0 all-to-all-start
  32.7 0.0 copy-done.1
  32.7 22.3 cosine_convert_fusion
  55.0 2.8 pad_maximum_fusion.1
  57.8 13.9 copy.49
  71.7 11.6 convert_element_type.43
  83.3 322.0 %all-to-all-done = bf16[160,50,3,640]{3,1,2,0:T(8,128)(2,1)} async-done(((bf16[160,50,3,640]{3,1,2,0:T(8,128)(2,1)}), bf16[160,50,3,640]{3,1,2,0:T(8,128)(2,1)}, u32[]{:S(2)}, u32[]{:S(2)}) %all-to-all-start) | async-done | bytes 30720032 | tf_op jit(solution)/shard_map/all_to_all | solution.py:31
  405.3 27.3 %copy.51 = bf16[4,40,50,3,640]{4,0,3,2,1:T(4,128)(2,1)} copy(bf16[4,40,50,3,640]{4,2,3,1,0:T(8,128)(2,1)} %bitcast.2) | data formatting | bytes 61440000 | tf_op jit(solution)/shard_map/all_to_all | solution.py:31
  432.6 21.6 copy.71
  454.1 39.4 %multiply_bitcast_fusion = f32[6000,1024]{1,0:T(8,128)} fusion(bf16[2560,1024]{0,1:T(8,128)(2,1)} %convert_element_type.43, bf16[6000,2560]{1,0:T(8,128)(2,1)} %bitcast.53), kind=kOutput, calls=%fused_computation.10 | convolution fusion | flops 31463424000 | bytes 60538880 | tf_op jit(solution)/shard_map/dot_general | solution.py:32
  493.5 19.6 mul.105
  513.2 43.5 %copy.52 = f32[40,150,1024]{1,0,2:T(8,128)} copy(f32[40,150,1024]{2,1,0:T(8,128)} %mul.105) | data formatting | bytes 49152000 | tf_op jit(solution)/shard_map/mul | solution.py:35
  556.7 915.9 %all_to_all.38 = f32[40,150,1024]{1,0,2:T(8,128)} all-to-all(f32[40,150,1024]{1,0,2:T(8,128)} %copy.52), channel_id=1, replica_groups=mesh['lat'=8,'lon'=4] {'lat'}, dimensions={2} | all-to-all | bytes 49152000 | tf_op jit(solution)/shard_map/all_to_all | solution.py:40
  1472.6 36.6 %copy.54 = f32[8,40,150,128]{3,1,0,2:T(8,128)} copy(f32[8,40,150,128]{2,1,3,0:T(8,128)} %bitcast.50) | data formatting | bytes 49152000 | tf_op jit(solution)/shard_map/all_to_all | solution.py:40
  1509.2 62.8 %slice_bitcast_fusion.3 = (f32[1,320,150,32]{3,1,2,0:T(8,128)}, f32[1,320,150,32]{3,1,2,0:T(8,128)}, f32[1,320,150,32]{3,1,2,0:T(8,128)}, f32[1,320,150,32]{3,1,2,0:T(8,128)}) fusion(f32[320,150,128]{2,0,1:T(8,128)} %bitcast.47), kind=kLoop, calls=%fused_computation.9 | loop fusion | bytes 49152000 | tf_op jit(solution)/shard_map/stack | solution.py:38
  1572.0 17.2 copy.55
  1589.2 17.2 copy.56
  1606.4 17.2 copy.57
  1623.6 17.2 copy.58
  1640.8 20.7 pad_maximum_fusion
  1661.5 0.0 copy-start
  1661.5 9.2 all-to-all-start.2
  1670.7 0.0 copy-done
  1670.7 0.1 mul.108
  1670.8 0.2 mul.109
  1671.0 0.8 compare_select_fusion
  1671.8 0.1 fusion.11
  1671.9 318.1 %all-to-all-done.2 = f32[4,320,150,32]{1,3,2,0:T(8,128)} async-done(((f32[4,320,150,32]{1,3,2,0:T(8,128)}), f32[4,320,150,32]{1,3,2,0:T(8,128)}, u32[]{:S(2)}, u32[]{:S(2)}) %all-to-all-start.2) | async-done | bytes 24576032 | tf_op jit(solution)/shard_map/all_to_all | solution.py:37
  1990.0 46.4 %copy.59 = f32[4,320,150,32]{2,3,1,0:T(8,128)} copy(f32[4,320,150,32]{1,3,2,0:T(8,128)} %all-to-all-done.2) | data formatting | bytes 49152000 | tf_op jit(solution)/shard_map/all_to_all | solution.py:37
  2036.4 39.1 %copy.60 = f32[8,4,40,150,32]{3,2,1,0,4:T(8,128)} copy(f32[8,4,40,150,32]{3,4,2,0,1:T(8,128)} %bitcast.51) | data formatting | bytes 49152000 | tf_op jit(solution)/shard_map/transpose | solution.py:52
  2075.5 76.9 %fusion = f32[16,640,150,2]{1,2,3,0:T(8,128)} fusion(f32[1280,150,16,2]{1,0,3,2:T(8,128)} %bitcast.49, bf16[16,1280,640]{2,1,0:T(8,128)(2,1)} %param.5, f32[16,640]{1,0:T(8,128)S(1)} %fusion.11), kind=kOutput, calls=%fused_computation | convolution fusion | flops 47212134400 | bytes 63119360 | tf_op jit(solution)/shard_map/aftp,tan->ftpn/dot_general | solution.py:62
  2152.4 10.6 copy.74
  2163.0 13.1 fusion.5
  2176.1 18.4 copy.64
  2194.5 15.2 mul.112
  2209.7 22.6 copy.63
  2232.3 15.1 reshape_reshape.11
  2247.4 16.2 fusion.12
  2263.6 39.1 %psum.7 = f32[50,50]{1,0:T(8,128)S(1)} all-reduce(f32[50,50]{1,0:T(8,128)S(1)} %fusion.12), channel_id=1, replica_groups=mesh['lat'=8,'lon'=4] {'lat','lon'}, use_global_device_ids=true, to_apply=%region_0.1 | all-reduce | flops 2500 | bytes 20000 | tf_op jit(solution)/shard_map/psum | solution.py:73
  2302.8 0.6 broadcast_multiply_fusion
  2303.4 10.1 copy.65
Async XLA Ops:
  22.7 10.0 copy-start.1
  22.7 382.6 %all-to-all-start = ((bf16[160,50,3,640]{3,1,2,0:T(8,128)(2,1)}), bf16[160,50,3,640]{3,1,2,0:T(8,128)(2,1)}, u32[]{:S(2)}, u32[]{:S(2)}) async-start(bf16[160,50,3,640]{3,1,2,0:T(8,128)(2,1)} %copy.50), calls=%async_computation | async-start | bytes 68812800 | tf_op jit(solution)/shard_map/all_to_all | solution.py:31
  1661.5 9.2 copy-start
  1661.5 328.5 %all-to-all-start.2 = ((f32[4,320,150,32]{1,3,2,0:T(8,128)}), f32[4,320,150,32]{1,3,2,0:T(8,128)}, u32[]{:S(2)}, u32[]{:S(2)}) async-start(f32[4,320,150,32]{1,3,2,0:T(8,128)} %pad_maximum_fusion), calls=%async_computation.2 | async-start | bytes 58982400 | tf_op jit(solution)/shard_map/all_to_all | solution.py:37
